TPU v7x, 32 devices: a whole 2x2x4 slice. The times are simulated.
32 devices in a mesh: fsdp: 4 (over x, core), context: 4 (over z), tensor: 2 (over y).
Axes of the slice: x: 2, y: 2, z: 4, core: 2. Of those that a mesh axis runs over, the one named last changes fastest.
Arguments:
- block_input: float32 [8192, 768], P(('fsdp', 'context')), may hold values from -18 to 18
- ln1_gain: float32 [768], replicated, may hold values from 0.1 to 1.9
- ln1_shift: float32 [768], replicated, may hold values from -3 to 3
- qkv_weight: float32 [768, 3, 768], P(('fsdp', 'context'), None, 'tensor'), may hold values from -0.21875 to 0.21875
- qkv_bias: float32 [3, 768], P(None, 'tensor'), may hold values from -3 to 3
- feat_query: float32 [12, 64, 64], P('tensor'), may hold values from -1.5 to 1.5
- feat_key: float32 [12, 64, 64], P('tensor'), may hold values from -1.5 to 1.5
- out_weight: float32 [768, 768], P('tensor', ('fsdp', 'context')), may hold values from -3.5 to 3.5
- out_bias: float32 [768], replicated, may hold values from -3 to 3
- ln2_gain: float32 [768], replicated, may hold values from 0.1 to 1.9
- ln2_shift: float32 [768], replicated, may hold values from -3 to 3
- up_weight: float32 [768, 3072], P(('fsdp', 'context'), 'tensor'), may hold values from -0.21875 to 0.21875
- up_bias: float32 [3072], P('tensor'), may hold values from -3 to 3
- down_weight: float32 [3072, 768], P('tensor', ('fsdp', 'context')), may hold values from -0.109375 to 0.109375
- down_bias: float32 [768], replicated, may hold values from -3 to 3
- lengths: int32 [4], replicated, may hold values from 1024 to 2048, as said below
- deal: int32 [128], P(('fsdp', 'context')), may hold values from 0 to 127, as said below
- cotangent: float32 [8192, 768], P(('fsdp', 'context')), may hold values from -6 to 6
Outputs:
- dealt_output: float32 [128, 64, 768], P(('fsdp', 'context'), 'tensor')
- rms: float32 [3], replicated
- grad_input: float32 [8192, 768], P(('fsdp', 'context'))
- grad_ln1_gain: float32 [768], replicated
- grad_ln1_shift: float32 [768], replicated
- grad_qkv_weight: float32 [768, 3, 768], P(('fsdp', 'context'), None, 'tensor')
- grad_qkv_bias: float32 [3, 768], P(None, 'tensor')
- grad_feat_query: float32 [12, 64, 64], P('tensor')
- grad_feat_key: float32 [12, 64, 64], P('tensor')
- grad_out_weight: float32 [768, 768], P('tensor', ('fsdp', 'context'))
- grad_out_bias: float32 [768], replicated
- grad_ln2_gain: float32 [768], replicated
- grad_ln2_shift: float32 [768], replicated
- grad_up_weight: float32 [768, 3072], P(('fsdp', 'context'), 'tensor')
- grad_up_bias: float32 [3072], P('tensor')
- grad_down_weight: float32 [3072, 768], P('tensor', ('fsdp', 'context'))
- grad_down_bias: float32 [768], replicated
Inputs may be any that keep to these rules, and one draw needn't show every extreme that they name: Sequence lengths; the 4 lengths sum to exactly 8160, and the last of them is exactly 2048. deal is a permutation of the 128 groups. Group j of the device with fsdp index f and context index e (groups numbered along fsdp, then context, then position) goes to position (f * 4 + d) * 8 + e * 2 + r, where the 8 groups of one device take every pair of d < 4 and r < 2 once.
All inputs are finite; a program needn't handle non-finite values.
Results may differ from a plain program's by a relative error of at most 0.0003.
Values sent between devices are 32-bit elements; how exact they have to be, the bound alone decides.
No kernel may reach another device: no remote copies, remote signals or barrier semaphores. Data moves between devices by JAX's collectives and lax.ppermute only.
A program may use at most 128 MiB of HBM per device.

v0:
```python
from functools import partial
import jax
import jax.numpy as jnp
from jax import lax
from jax.sharding import PartitionSpec as P

HIGH = lax.Precision.HIGHEST
NORM_EPS = 1e-05


def entering(x, axis, combine, identity, reverse):
    count, place = (lax.axis_size(axis), lax.axis_index(axis))
    everything = jax.tree.map(lambda part: lax.all_gather(part, axis), x)
    start = jax.tree.map(
        lambda part, zero: jnp.broadcast_to(jnp.asarray(zero, part.dtype), part.shape), x, identity
    )

    def lap(k, before):
        at = count - 1 - k if reverse else k
        reached = at > place if reverse else at < place
        new = combine(before, jax.tree.map(lambda part: part[at], everything))
        return jax.tree.map(lambda a, b: jnp.where(reached, a, b), new, before)

    return lax.fori_loop(0, count, lap, start)


def layer_norm(values, gain, shift):
    middle = jnp.mean(values, axis=-1, keepdims=True)
    centred = values - middle
    spread = jnp.mean(centred * centred, axis=-1, keepdims=True)
    return centred * lax.rsqrt(spread + NORM_EPS) * gain + shift


def feature_map(heads, weight):
    logits = jnp.einsum("rhd,hde->rhe", heads, weight, precision=HIGH)
    return jnp.concatenate(
        [jax.nn.softmax(logits, axis=-1), jax.nn.softmax(-logits, axis=-1)], axis=-1
    )


def segment_of(places, ends, total, number):
    found = jnp.sum((ends[None, :] <= places[:, None]).astype(jnp.int32), axis=1)
    found = jnp.where(places < 0, -1, found)
    return jnp.where(places >= total, number + 1, found)


def project(normed, weight, bias):
    return jnp.einsum("rd,dke->rke", normed, weight, precision=HIGH) + bias


def mlp_part(normed, up_full, up_bias, down_full):
    active = jax.nn.gelu(jnp.dot(normed, up_full, precision=HIGH) + up_bias, approximate=True)
    return jnp.dot(active, down_full, precision=HIGH)


def chain_join(earlier, later):
    passing = 1.0 - later[2]
    return (
        later[0] + passing * earlier[0],
        later[1] + passing * earlier[1],
        jnp.maximum(earlier[2], later[2]),
    )


def local_part(queries, keys, values, weight_q, weight_k, segment, seg_first, block):
    phi_q = feature_map(queries, weight_q)
    phi_k = feature_map(keys, weight_k)
    count_rows, local_heads, head_dim = values.shape
    feats = phi_q.shape[2]
    blocks = count_rows // block
    lower = jnp.arange(block)[:, None] >= jnp.arange(block)[None, :]

    def block_step(carry, pieces):
        state, normer, seg_carry = carry
        piece_q, piece_k, piece_v, seg_piece = pieces
        allowed = jnp.logical_and(lower, seg_piece[:, None] == seg_piece[None, :]).astype(
            jnp.float32
        )
        scores = jnp.einsum("ihf,jhf->hij", piece_q, piece_k, precision=HIGH) * allowed[None]
        numer = jnp.einsum("hij,jhd->ihd", scores, piece_v, precision=HIGH)
        denom = jnp.einsum("hij->ih", scores)
        carried = (seg_piece == seg_carry).astype(jnp.float32)
        numer = numer + carried[:, None, None] * jnp.einsum(
            "ihf,hfd->ihd", piece_q, state, precision=HIGH
        )
        denom = denom + carried[:, None] * jnp.einsum("ihf,hf->ih", piece_q, normer, precision=HIGH)
        final_seg = seg_piece[-1]
        stays = (final_seg == seg_carry).astype(jnp.float32)
        tail_k = piece_k * (seg_piece == final_seg).astype(jnp.float32)[:, None, None]
        state = stays * state + jnp.einsum("jhf,jhd->hfd", tail_k, piece_v, precision=HIGH)
        normer = stays * normer + jnp.sum(tail_k, axis=0)
        return ((state, normer, final_seg), (numer, denom))

    def blocked(array):
        return array.reshape((blocks, block) + array.shape[1:])

    start = (
        jnp.zeros((local_heads, feats, head_dim), jnp.float32),
        jnp.zeros((local_heads, feats), jnp.float32),
        seg_first,
    )
    (state, normer, _), (numer, denom) = lax.scan(
        jax.checkpoint(block_step),
        start,
        (blocked(phi_q), blocked(phi_k), blocked(values), blocked(segment)),
    )
    return (
        phi_q,
        numer.reshape(count_rows, local_heads, head_dim),
        denom.reshape(count_rows, local_heads),
        state,
        normer,
    )


def body(
    block_input,
    ln1_gain,
    ln1_shift,
    qkv_weight,
    qkv_bias,
    feat_query,
    feat_key,
    out_weight,
    out_bias,
    ln2_gain,
    ln2_shift,
    up_weight,
    up_bias,
    down_weight,
    down_bias,
    lengths,
    deal,
    cotangent,
):
    count_rows, width = block_input.shape
    local_heads, head_dim = (feat_query.shape[0], feat_query.shape[1])
    local_width = local_heads * head_dim
    offset = lax.axis_index(("fsdp", "context")) * count_rows
    total = count_rows * lax.axis_size(("fsdp", "context"))
    ends = jnp.cumsum(lengths)
    used = ends[-1]
    number = lengths.shape[0]
    places = offset + jnp.arange(count_rows, dtype=jnp.int32)
    segment = segment_of(places, ends, total, number)
    edges = segment_of(offset + jnp.array([-1, count_rows], dtype=jnp.int32), ends, total, number)
    seg_first = segment[0]
    seg_final = segment[-1]
    carry_in = (edges[0] == seg_first).astype(jnp.float32)
    breaks = (edges[0] != seg_final).astype(jnp.float32)
    valid = (places < used).astype(jnp.float32)[:, None]
    block = min(512, count_rows)
    qkv_full, out_full, up_full, down_full = (
        lax.all_gather(qkv_weight, ("fsdp", "context"), axis=0, tiled=True),
        lax.all_gather(out_weight, ("fsdp", "context"), axis=1, tiled=True),
        lax.all_gather(up_weight, ("fsdp", "context"), axis=0, tiled=True),
        lax.all_gather(down_weight, ("fsdp", "context"), axis=1, tiled=True),
    )
    normed1 = layer_norm(block_input, ln1_gain, ln1_shift)
    qkv = project(normed1, qkv_full, qkv_bias)
    queries = qkv[:, 0, :].reshape(count_rows, local_heads, head_dim)
    keys = qkv[:, 1, :].reshape(count_rows, local_heads, head_dim)
    values = qkv[:, 2, :].reshape(count_rows, local_heads, head_dim)
    attend_local = partial(local_part, segment=segment, seg_first=seg_first, block=block)
    phi_q, numer_local, denom_local, state_tail, norm_tail = attend_local(
        queries, keys, values, feat_query, feat_key
    )
    identity = (jnp.zeros_like(state_tail), jnp.zeros_like(norm_tail), jnp.zeros((), jnp.float32))
    state_scan, norm_scan, _ = entering(
        (state_tail, norm_tail, breaks), ("fsdp", "context"), chain_join, identity, False
    )
    state_in = carry_in * state_scan
    norm_in = carry_in * norm_scan
    first_rows = (segment == seg_first).astype(jnp.float32)[:, None, None]
    masked_q = phi_q * first_rows
    numer = numer_local + jnp.einsum("rhf,hfd->rhd", masked_q, state_in, precision=HIGH)
    denom = denom_local + jnp.einsum("rhf,hf->rh", masked_q, norm_in, precision=HIGH)
    attended = numer / denom[:, :, None]
    attended_flat = attended.reshape(count_rows, local_width)
    attn_part = jnp.dot(attended_flat, out_full, precision=HIGH)
    attn = lax.psum(attn_part, "tensor") + out_bias
    hidden = block_input + attn
    normed2 = layer_norm(hidden, ln2_gain, ln2_shift)
    slots = deal.shape[0]
    group_rows = count_rows // slots
    part_rows = group_rows // lax.axis_size("tensor")
    part_start = lax.axis_index("tensor") * part_rows
    per_peer = slots // lax.axis_size("context")
    slot_of = deal // slots % lax.axis_size("context") * per_peer + deal % per_peer
    counting = jnp.arange(slots, dtype=jnp.int32)
    source_of = jnp.sum(
        jnp.where(slot_of[None, :] == counting[:, None], counting[None, :], 0), axis=1
    )
    mlp_terms = mlp_part(normed2, up_full, up_bias, down_full)
    mlp = lax.psum(mlp_terms, "tensor") + down_bias
    result = hidden + mlp
    outbound = jnp.take(result.reshape(slots, group_rows, width), source_of, axis=0)
    dealt_whole = lax.all_to_all(outbound, "context", split_axis=0, concat_axis=0, tiled=True)
    dealt_output = lax.dynamic_slice_in_dim(dealt_whole, part_start, part_rows, 1)
    squares = jnp.stack(
        [jnp.sum(valid * result * result), jnp.sum(valid * attn * attn), jnp.sum(valid * mlp * mlp)]
    )
    inbound = lax.all_to_all(
        cotangent.reshape(slots, group_rows, width),
        "context",
        split_axis=0,
        concat_axis=0,
        tiled=True,
    )
    grad_y = jnp.take(inbound, slot_of, axis=0).reshape(count_rows, width) * valid
    grad_down_bias = jnp.sum(grad_y, axis=0)
    _, mlp_backward = jax.vjp(mlp_part, normed2, up_full, up_bias, down_full)
    grad_normed2_part, grad_up_full, grad_up_bias, grad_down_full = mlp_backward(grad_y)
    grad_normed2 = lax.psum(grad_normed2_part, "tensor")
    _, norm2_backward = jax.vjp(layer_norm, hidden, ln2_gain, ln2_shift)
    grad_hidden_norm, grad_ln2_gain, grad_ln2_shift = norm2_backward(grad_normed2)
    grad_hidden = grad_y + grad_hidden_norm
    grad_out_bias = jnp.sum(grad_hidden, axis=0)
    grad_out_full = jnp.einsum("rd,re->de", attended_flat, grad_hidden, precision=HIGH)
    grad_attended = jnp.einsum("re,de->rd", grad_hidden, out_full, precision=HIGH).reshape(
        count_rows, local_heads, head_dim
    )
    grad_numer = grad_attended / denom[:, :, None]
    grad_denom = -jnp.sum(grad_attended * attended, axis=2) / denom
    grad_state_in = carry_in * jnp.einsum("rhf,rhd->hfd", masked_q, grad_numer, precision=HIGH)
    grad_norm_in = carry_in * jnp.einsum("rhf,rh->hf", masked_q, grad_denom, precision=HIGH)
    grad_phi_extra = first_rows * (
        jnp.einsum("rhd,hfd->rhf", grad_numer, state_in, precision=HIGH)
        + grad_denom[:, :, None] * norm_in[None, :, :]
    )
    grad_state_tail, grad_norm_tail, _ = entering(
        (grad_state_in, grad_norm_in, breaks), ("fsdp", "context"), chain_join, identity, True
    )
    _, attention_backward = jax.vjp(attend_local, queries, keys, values, feat_query, feat_key)
    grad_queries, grad_keys, grad_values, grad_feat_query, grad_feat_key = attention_backward(
        (grad_phi_extra, grad_numer, grad_denom, grad_state_tail, grad_norm_tail)
    )
    grad_qkv = jnp.stack(
        [
            grad_queries.reshape(count_rows, local_width),
            grad_keys.reshape(count_rows, local_width),
            grad_values.reshape(count_rows, local_width),
        ],
        axis=1,
    )
    _, project_backward = jax.vjp(project, normed1, qkv_full, qkv_bias)
    grad_normed1_part, grad_qkv_full, grad_qkv_bias = project_backward(grad_qkv)
    grad_normed1 = lax.psum(grad_normed1_part, "tensor")
    _, norm1_backward = jax.vjp(layer_norm, block_input, ln1_gain, ln1_shift)
    grad_input_norm, grad_ln1_gain, grad_ln1_shift = norm1_backward(grad_normed1)
    grad_input = grad_hidden + grad_input_norm
    grad_qkv_weight, grad_out_weight, grad_up_weight, grad_down_weight = (
        lax.psum_scatter(grad_qkv_full, ("fsdp", "context"), scatter_dimension=0, tiled=True),
        lax.psum_scatter(grad_out_full, ("fsdp", "context"), scatter_dimension=1, tiled=True),
        lax.psum_scatter(grad_up_full, ("fsdp", "context"), scatter_dimension=0, tiled=True),
        lax.psum_scatter(grad_down_full, ("fsdp", "context"), scatter_dimension=1, tiled=True),
    )
    summed = lax.psum(
        (
            grad_ln1_gain,
            grad_ln1_shift,
            grad_qkv_bias,
            grad_feat_query,
            grad_feat_key,
            grad_out_bias,
            grad_ln2_gain,
            grad_ln2_shift,
            grad_up_bias,
            grad_down_bias,
            squares,
        ),
        ("fsdp", "context"),
    )
    rms = jnp.sqrt(summed[10] / (used.astype(jnp.float32) * width))
    return (
        dealt_output,
        rms,
        grad_input,
        summed[0],
        summed[1],
        grad_qkv_weight,
        summed[2],
        summed[3],
        summed[4],
        grad_out_weight,
        summed[5],
        summed[6],
        summed[7],
        grad_up_weight,
        summed[8],
        grad_down_weight,
        summed[9],
    )


def solution(mesh):
    in_specs = (
        P(("fsdp", "context"), None),
        P(),
        P(),
        P(("fsdp", "context"), None, "tensor"),
        P(None, "tensor"),
        P("tensor", None, None),
        P("tensor", None, None),
        P("tensor", ("fsdp", "context")),
        P(),
        P(),
        P(),
        P(("fsdp", "context"), "tensor"),
        P("tensor"),
        P("tensor", ("fsdp", "context")),
        P(),
        P(),
        P(("fsdp", "context")),
        P(("fsdp", "context"), None),
    )
    out_specs = (
        P(("fsdp", "context"), "tensor", None),
        P(),
        P(("fsdp", "context"), None),
        P(),
        P(),
        P(("fsdp", "context"), None, "tensor"),
        P(None, "tensor"),
        P("tensor", None, None),
        P("tensor", None, None),
        P("tensor", ("fsdp", "context")),
        P(),
        P(),
        P(),
        P(("fsdp", "context"), "tensor"),
        P("tensor"),
        P("tensor", ("fsdp", "context")),
        P(),
    )
    return jax.shard_map(body, mesh=mesh, in_specs=in_specs, out_specs=out_specs, check_vma=False)
```

profile of v0, /device:TPU:0, one launch (start us, length us, event | category | flops | bytes accessed | tf_op | source)
XLA Modules:
  0.0 1227.2 jit_solution(8723379923862665840)
XLA Ops:
  13.2 47.0 %all-gather.13.cloned.1.call-done = f32[768,3,384]{2,0,1:T(8,128)} async-done(((f32[48,3,384]{2,0,1:T(8,128)}), f32[768,3,384]{2,0,1:T(8,128)}) %all-gather.13.cloned.1.call-update) | async-done | bytes 3538960 | tf_op jit(solution)/shard_map/all_gather | solution.py:154
  60.3 8.5 convolution_add_fusion.1
  82.2 43.4 %all-reduce = f32[16]{0:T(128)} all-reduce(f32[16]{0:T(128)S(1)} %dynamic-update-slice), channel_id=1, replica_groups=mesh['fsdp'=4,'context'=4,'tensor'=2] {'fsdp','context'}, use_global_device_ids=true, to_apply=%add | all-reduce | flops 16 | bytes 128
  130.5 31.8 %all-gather.4 = f32[16,6,128]{2,1,0:T(8,128)} all-gather(f32[1,6,128]{2,1,0:T(8,128)S(1)} %bitcast.196), channel_id=3, replica_groups=mesh['fsdp'=4,'context'=4,'tensor'=2] {'fsdp','context'}, dimensions={0}, use_global_device_ids=true | all-gather | bytes 52224 | tf_op jit(solution)/shard_map/all_gather | solution.py:13
  165.9 8.0 multiply_reduce_fusion
  174.0 111.7 %while.22 = (s32[]{:T(128)}, f32[6,128,64]{2,1,0:T(8,128)}, f32[6,128]{1,0:T(8,128)}, s32[]{:T(128)}, f32[16,6,128,64]{2,3,1,0:T(8,128)}, /*index=5*/f32[16]{0:T...) while((s32[]{:T(128)}, f32[6,128,64]{2,1,0:T(8,128)}, f32[6,128]{1,0:T(8,128)}, ...), condition=%wide.region_15.16_spmd.clone, body=%wide.region_14.15_spmd.clone.sunk | while | flops 199685 | bytes 1385643 | solution.py:24
  290.9 6.3 fusion.59
  297.2 6.6 fusion.167
  310.1 33.8 %all-to-all-done.1 = f32[8,64,768]{2,1,0:T(8,128)S(1)} async-done(((f32[8,64,768]{2,1,0:T(8,128)}), f32[8,64,768]{2,1,0:T(8,128)S(1)}, u32[]{:S(2)}, u32[]{:S(2)}) %all-to-all-start.1) | async-done | bytes 1572896 | tf_op jit(solution)/shard_map/all_to_all | solution.py:203
  349.3 11.4 fusion.168
  362.8 47.3 %all-gather.17.cloned.1.call-done = f32[768,1536]{1,0:T(8,128)} async-done(((f32[48,1536]{1,0:T(8,128)}), f32[768,1536]{1,0:T(8,128)}) %all-gather.17.cloned.1.call-update) | async-done | bytes 4718608 | tf_op jit(solution)/shard_map/all_gather | solution.py:156
  410.1 14.9 %fusion.155 = (f32[1536]{0:T(1024)}, f32[512,1536]{1,0:T(8,128)S(1)}, f32[512,1536]{1,0:T(8,128)}) fusion(f32[512,1536]{1,0:T(8,128)} %fusion.168, f32[1536]{0:T(1024)S(1)} %copy-done.118, f32[768,1536]{1,0:T(8,128)} %all-gather.17.cloned.1.call-done, f32[512,768]{1,0:T(8,128)S(1)} %get-tuple-element.631, f32[768]{0:T(1024)S(1)} %copy-done.83, ...), kind=kOutput, calls=%fused_computation.257 | convolution fusion | flops 7265843712 | bytes 15751168 | tf_op jit(solution)/shard_map/dot_general | solution.py:52
  426.6 9.0 fusion.169
  435.9 50.0 %all-reduce.11.cloned.1.call-done = f32[512,768]{1,0:T(8,128)} async-done(((f32[512,768]{1,0:T(8,128)}), f32[512,768]{1,0:T(8,128)}) %all-reduce.11.cloned.1.call-update) | async-done | bytes 1572880 | tf_op jit(solution)/shard_map/psum | solution.py:214
  503.5 12.7 %fusion.38 = f32[512,768]{1,0:T(8,128)} fusion(f32[1536,768]{0,1:T(8,128)} %all-gather.19.cloned.1.call-done, f32[512,1536]{1,0:T(8,128)S(1)} %copy-done.124), kind=kOutput, calls=%fused_computation.80 | convolution fusion | flops 7254048768 | bytes 9437184 | tf_op jit(solution)/shard_map/dot_general | solution.py:53
  517.7 35.5 %all-gather.5 = f32[16,6,128]{2,1,0:T(8,128)} all-gather(f32[1,6,128]{2,1,0:T(8,128)S(1)} %fusion.126), channel_id=5, replica_groups=mesh['fsdp'=4,'context'=4,'tensor'=2] {'fsdp','context'}, dimensions={0}, use_global_device_ids=true | all-gather | bytes 52224 | tf_op jit(solution)/shard_map/all_gather | solution.py:13
  553.3 111.7 %while.23 = (s32[]{:T(128)}, f32[6,128,64]{2,1,0:T(8,128)}, f32[6,128]{1,0:T(8,128)}, s32[]{:T(128)}, f32[16,6,128,64]{2,3,1,0:T(8,128)}, /*index=5*/f32[16]{0:T...) while((s32[]{:T(128)}, f32[6,128,64]{2,1,0:T(8,128)}, ...), condition=%wide.region_31.33_spmd.clone, body=%wide.region_30.32_spmd.clone.sunk | while | flops 199689 | bytes 1385705 | solution.py:24
  671.0 7.3 fusion.171
  678.4 5.1 fusion.88
  683.6 5.3 fusion.12
  688.9 8.5 fusion.13
  727.5 10.4 convolution_bitcast_fusion
  738.0 5.4 fusion.172
  743.5 12.1 fusion.62
  755.6 12.1 fusion.37
  772.7 10.1 fusion.30
  783.6 37.0 %all-reduce.15.cloned.1.call-done = (f32[512,768]{1,0:T(8,128)}, f32[512,768]{1,0:T(8,128)}) async-done(((f32[512,768]{1,0:T(8,128)}, f32[512,768]{1,0:T(8,128)}), (f32[512,768]{1,0:T(8,128)}, f32[512,768]{1,0:T(8,128)})) %all-reduce.15.cloned.1.call-update) | async-done | bytes 3145744 | tf_op jit(solution)/shard_map/psum | solution.py:195
  837.8 89.3 %all-reduce.1 = (f32[3]{0:T(128)S(1)}, f32[768]{0:T(1024)}, f32[768]{0:T(1024)}, f32[3,384]{1,0:T(4,128)}, f32[768]{0:T(1024)}, /*index=5*/f32[768]{0:T(1024)}, f32[768]{0:T(1024)}, f32[1536]{0:T(1024)}, f32[768]{0:T(1024)}) all-reduce(f32[3]{0:T(128)S(1)} %pad_maximum_fusion.5, ...), channel_id=1, replica_groups=mesh['fsdp'=4,'context'=4,'tensor'=2] {'fsdp','context'}, use_global_device_ids=true, to_apply=%region_25.27 | all-reduce | flops 7299 | bytes 58392 | tf_op jit(solution)/shard_map/psum | solution.py:258
  932.4 38.8 %reduce-scatter.9.cloned.1.call-done = f32[48,1536]{1,0:T(8,128)} async-done(((f32[768,1536]{1,0:T(8,128)}), f32[48,1536]{1,0:T(8,128)}) %reduce-scatter.9.cloned.1.call-update) | async-done | bytes 294928 | tf_op jit(solution)/shard_map/reduce_scatter | solution.py:255
  971.2 79.1 %reduce-scatter.11.cloned.1.call-done = f32[1536,48]{0,1:T(8,128)} async-done(((f32[1536,768]{0,1:T(8,128)}), f32[1536,48]{0,1:T(8,128)}) %reduce-scatter.11.cloned.1.call-update) | async-done | bytes 294928 | tf_op jit(solution)/shard_map/reduce_scatter | solution.py:256
  1050.3 95.4 %all-reduce.13.cloned.1.call-done = (f32[6,64,64]{2,1,0:T(8,128)}, f32[6,64,64]{2,1,0:T(8,128)}) async-done(((f32[6,64,64]{2,1,0:T(8,128)}, f32[6,64,64]{2,1,0:T(8,128)}), (f32[6,64,64]{2,1,0:T(8,128)}, f32[6,64,64]{2,1,0:T(8,128)})) %all-reduce.13.cloned.1.call-update) | async-done | bytes 196624 | tf_op jit(solution)/shard_map/psum | solution.py:258
  1145.7 71.5 %reduce-scatter.5.cloned.1.call-done = f32[48,3,384]{2,0,1:T(8,128)} async-done(((f32[768,3,384]{2,0,1:T(8,128)}), f32[48,3,384]{2,0,1:T(8,128)}) %reduce-scatter.5.cloned.1.call-update) | async-done | bytes 221200 | tf_op jit(solution)/shard_map/reduce_scatter | solution.py:253
  (560 shorter events, 334.5 us)
Async XLA Ops:
  7.2 62.7 %copy-start = (f32[6,64,64]{2,1,0:T(8,128)S(1)}, f32[6,64,64]{2,1,0:T(8,128)}, u32[]{:S(2)}) copy-start(f32[6,64,64]{2,1,0:T(8,128)} %param.31) | copy-start | bytes 294916
  7.2 53.1 %all-gather.13.cloned.1.call-start = ((), (), s32[]{:S(2)}) async-start(), calls=%async_computation.6 | async-start | bytes 3760128 | tf_op jit(solution)/shard_map/all_gather | solution.py:154
  8.0 166.0 %all-gather.21.cloned.1.call-start = ((), (), s32[]{:S(2)}) async-start(), calls=%async_computation.16 | async-start | bytes 3342336 | tf_op jit(solution)/shard_map/all_gather | solution.py:13
  8.8 70.6 %copy-start.114 = (s32[4,1]{0,1:T(1,128)}, s32[4,1]{0,1:T(1,128)S(1)}, u32[]{:S(2)}) copy-start(s32[4,1]{0,1:T(1,128)S(1)} %reduce-window.4) | copy-start | bytes 52
  10.5 67.7 %copy-start.79 = (s32[512]{0:T(512)}, s32[512]{0:T(512)S(1)}, u32[]{:S(2)}) copy-start(s32[512]{0:T(512)S(1)} %select_select_fusion) | copy-start | bytes 6148
  11.1 57.6 %copy-start.92 = (f32[512]{0:T(512)}, f32[512]{0:T(512)S(1)}, u32[]{:S(2)}) copy-start(f32[512]{0:T(512)S(1)} %broadcast_multiply_fusion.2) | copy-start | bytes 6148
  11.5 57.3 %copy-start.99 = (f32[512]{0:T(512)}, f32[512]{0:T(512)S(1)}, u32[]{:S(2)}) copy-start(f32[512]{0:T(512)S(1)} %fusion.133) | copy-start | bytes 6148
  13.2 150.8 %copy-start.75 = (f32[512]{0:T(512)}, f32[512]{0:T(512)S(1)}, u32[]{:S(2)}) copy-start(f32[512]{0:T(512)S(1)} %get-tuple-element.642) | copy-start | bytes 6148
  72.0 429.7 %copy-start.58 = (f32[512,6]{0,1:T(8,128)}, f32[512,6]{0,1:T(8,128)S(1)}, u32[]{:S(2)}) copy-start(f32[512,6]{0,1:T(8,128)S(1)} %get-tuple-element.645) | copy-start | bytes 36868
  74.1 51.5 %copy-start.24 = (f32[512,6,64]{0,2,1:T(8,128)}, f32[512,6,64]{0,2,1:T(8,128)S(1)}, u32[]{:S(2)}) copy-start(f32[512,6,64]{0,2,1:T(8,128)S(1)} %get-tuple-element.656) | copy-start | bytes 2359300
  74.1 51.5 %copy-start.26 = (f32[512,6,64]{0,2,1:T(8,128)}, f32[512,6,64]{0,2,1:T(8,128)S(1)}, u32[]{:S(2)}) copy-start(f32[512,6,64]{0,2,1:T(8,128)S(1)} %get-tuple-element.657) | copy-start | bytes 2359300
  76.8 220.4 %all-gather.15.cloned.1.call-start = ((), (), s32[]{:S(2)}) async-start(), calls=%async_computation.7 | async-start | bytes 1253376 | tf_op jit(solution)/shard_map/all_gather | solution.py:155
  77.6 271.8 %all-gather.19.cloned.1.call-start = ((), (), s32[]{:S(2)}) async-start(), calls=%async_computation.10 | async-start | bytes 5013504 | tf_op jit(solution)/shard_map/all_gather | solution.py:157
  78.1 282.6 %all-reduce.9.cloned.1.call-start = ((), (), s32[]{:S(2)}) async-start(), calls=%async_computation.8 | async-start | bytes 3145728 | tf_op jit(solution)/shard_map/psum | solution.py:181
  162.6 126.7 %copy-start.2 = (f32[512,6,64]{0,2,1:T(8,128)}, f32[512,6,64]{0,2,1:T(8,128)S(1)}, u32[]{:S(2)}) copy-start(f32[512,6,64]{0,2,1:T(8,128)S(1)} %get-tuple-element.658) | copy-start | bytes 2359300
  162.6 126.7 %copy-start.5 = (f32[512,6,64]{0,2,1:T(8,128)}, f32[512,6,64]{0,2,1:T(8,128)S(1)}, u32[]{:S(2)}) copy-start(f32[512,6,64]{0,2,1:T(8,128)S(1)} %get-tuple-element.659) | copy-start | bytes 2359300
  303.8 106.3 %all-gather.17.cloned.1.call-start = ((), (), s32[]{:S(2)}) async-start(), calls=%async_computation.9 | async-start | bytes 5013504 | tf_op jit(solution)/shard_map/all_gather | solution.py:156
  304.4 39.4 %all-to-all-start.1 = ((f32[8,64,768]{2,1,0:T(8,128)}), f32[8,64,768]{2,1,0:T(8,128)S(1)}, u32[]{:S(2)}, u32[]{:S(2)}) async-start(f32[8,64,768]{2,1,0:T(8,128)} %bitcast.190), calls=%async_computation.1 | async-start | bytes 3145728 | tf_op jit(solution)/shard_map/all_to_all | solution.py:203
  308.0 177.9 %all-reduce.11.cloned.1.call-start = ((), (), s32[]{:S(2)}) async-start(), calls=%async_computation.11 | async-start | bytes 3145728 | tf_op jit(solution)/shard_map/psum | solution.py:214
  309.3 180.0 %copy-start.97 = (f32[512]{0:T(512)}, f32[512]{0:T(512)S(1)}, u32[]{:S(2)}) copy-start(f32[512]{0:T(512)S(1)} %fusion.132) | copy-start | bytes 6148
  362.5 126.2 %copy-start.81 = (f32[512]{0:T(512)}, f32[512]{0:T(512)S(1)}, u32[]{:S(2)}) copy-start(f32[512]{0:T(512)S(1)} %broadcast_multiply_fusion.1) | copy-start | bytes 6148
  362.8 125.9 %copy-start.90 = (f32[512]{0:T(512)}, f32[512]{0:T(512)S(1)}, u32[]{:S(2)}) copy-start(f32[512]{0:T(512)S(1)} %fusion.134) | copy-start | bytes 6148
  435.7 117.6 %all-gather.23.cloned.1.call-start = ((), (), s32[]{:S(2)}) async-start(), calls=%async_computation.17 | async-start | bytes 3342336 | tf_op jit(solution)/shard_map/all_gather | solution.py:13
  497.9 322.7 %all-reduce.15.cloned.1.call-start = ((), (), s32[]{:S(2)}) async-start(), calls=%async_computation.19 | async-start | bytes 6291456 | tf_op jit(solution)/shard_map/psum | solution.py:195
  737.9 194.5 %reduce-scatter.7.cloned.1.call-start = ((), (), s32[]{:S(2)}) async-start(), calls=%async_computation.13 | async-start | bytes 1253376 | tf_op jit(solution)/shard_map/reduce_scatter | solution.py:254
  743.4 227.8 %reduce-scatter.9.cloned.1.call-start = ((), (), s32[]{:S(2)}) async-start(), calls=%async_computation.14 | async-start | bytes 5013504 | tf_op jit(solution)/shard_map/reduce_scatter | solution.py:255
  755.6 294.7 %reduce-scatter.11.cloned.1.call-start = ((), (), s32[]{:S(2)}) async-start(), calls=%async_computation.15 | async-start | bytes 5013504 | tf_op jit(solution)/shard_map/reduce_scatter | solution.py:256
  767.8 377.9 %all-reduce.13.cloned.1.call-start = ((), (), s32[]{:S(2)}) async-start(), calls=%async_computation.18 | async-start | bytes 786432 | tf_op jit(solution)/shard_map/psum | solution.py:258
  772.4 444.8 %reduce-scatter.5.cloned.1.call-start = ((), (), s32[]{:S(2)}) async-start(), calls=%async_computation.12 | async-start | bytes 3760128 | tf_op jit(solution)/shard_map/reduce_scatter | solution.py:253
  828.1 102.2 %all-to-all-start = ((f32[8,64,768]{2,1,0:T(8,128)}), f32[8,64,768]{2,1,0:T(8,128)}, u32[]{:S(2)}, u32[]{:S(2)}) async-start(f32[8,64,768]{2,1,0:T(8,128)} %broadcast_select_fusion.1), calls=%async_computation | async-start | bytes 3145728 | tf_op jit(solution)/shard_map/all_to_all | solution.py:198
  837.0 90.5 %copy-start.102 = (f32[512]{0:T(512)S(1)}, f32[512]{0:T(512)}, u32[]{:S(2)}) copy-start(f32[512]{0:T(512)} %copy-done.101) | copy-start | bytes 6148
  837.0 90.5 %copy-start.49 = (f32[512,768]{1,0:T(8,128)S(1)}, f32[512,768]{1,0:T(8,128)}, u32[]{:S(2)}) copy-start(f32[512,768]{1,0:T(8,128)} %get-tuple-element.616) | copy-start | bytes 4718596
  (109 other events, 900.3 us)
Sparse Core Ops, SparseCore 0:
  10.4 49.8 all-gather.12
  76.9 44.2 all-gather.20
  123.5 36.9 all-gather.14
  162.7 51.7 all-gather.18
  304.0 50.9 all-reduce.8
  357.1 52.9 all-gather.16
  435.8 50.0 all-reduce.10
  498.0 45.7 all-gather.22
  738.0 82.5 all-reduce.14
  824.7 67.4 reduce-scatter.6
  896.6 74.5 reduce-scatter.8
  975.5 74.7 reduce-scatter.10
  1054.9 90.7 all-reduce.12
  1150.0 67.1 reduce-scatter.4
where the time goes:
time: 1240 us; the launch traced here: 1230 us
  waiting for transfers between devices  503 us (41%)
  blocking collectives  200 us (16%)
  matrix products  192 us (15%)
  other arithmetic  149 us (12%)
  local copies, waits for them, and re-layouts  136 us (11%)
  loops' own time  21.4 us (2%)
  between operations  17.7 us (1%)
    select_n x64, other arithmetic, lap(): return jax.tree.map(lambda a, b: jnp.where(reached, a, b), new, before)  103 us
    dynamic_slice x96, local copies, waits for them, and re-layouts, lap(): new = combine(before, jax.tree.map(lambda part: part[at], everything))  99.5 us
    psum x1, waiting for transfers between devices, body(): lax.psum((grad_ln1_gain, grad_ln1_shift, grad_qkv_bias, grad_feat_query,...  95.4 us
    psum x1, blocking collectives, body(): lax.psum((grad_ln1_gain, grad_ln1_shift, grad_qkv_bias, grad_feat_query,...  89.3 us
    reduce_scatter x1, waiting for transfers between devices, body(): lax.psum_scatter(grad_down_full, ('fsdp', 'context'), scatter_dimension=1...  79.1 us
    reduce_scatter x1, waiting for transfers between devices, body(): lax.psum_scatter(grad_qkv_full, ('fsdp', 'context'), scatter_dimension=0,...  71.5 us
    all_gather x2, blocking collectives, entering(): everything = jax.tree.map(lambda part: lax.all_gather(part, axis), x)  67.3 us
    psum x1, waiting for transfers between devices, body(): grad_normed2 = lax.psum(grad_normed2_part, 'tensor')  50 us
  transfers between devices with their start and end apart: 16, of which 9 were waited for; matrix products, arithmetic and copies ran while one was open for 20% of the time, Pallas kernels for 0%

commit v1 on v0

--- a/solution.py
+++ b/solution.py
@@ -192,7 +192,7 @@
         jnp.where(slot_of[None, :] == counting[:, None], counting[None, :], 0), axis=1
     )
     mlp_terms = mlp_part(normed2, up_full, up_bias, down_full)
-    mlp = lax.psum(mlp_terms, "tensor") + down_bias
+    mlp = lax.all_gather(mlp_terms, axis_name="tensor").sum(axis=0) + down_bias
     result = hidden + mlp
     outbound = jnp.take(result.reshape(slots, group_rows, width), source_of, axis=0)
     dealt_whole = lax.all_to_all(outbound, "context", split_axis=0, concat_axis=0, tiled=True)

time: 1240 us -> 1240 us (level)
  blocking collectives: 200 us -> 159 us
  waiting for transfers between devices: 503 us -> 531 us
    all_gather x0 -> x1, waiting for transfers between devices: none -> 43.9 us  [body(): mlp = lax.all_gather(mlp_terms, axis_name='tensor').sum(axis=0) + down_bias]
    all_to_all x1, waiting for transfers between devices: 0.01 us -> 39.9 us  [body(): lax.all_to_all(outbound, 'context', split_axis=0, concat_axis=0, tiled=True)]
    psum x1, waiting for transfers between devices: 37 us -> 0.02 us  [body(): grad_normed1 = lax.psum(grad_normed1_part, 'tensor')]
    psum x1, blocking collectives: 89.3 us -> 59.3 us  [body(): lax.psum((grad_ln1_gain, grad_ln1_shift, grad_qkv_bias, grad_feat_query,...]
  transfers between devices with their start and end apart: 16 -> 17, of which waited for: 9 -> 11; matrix products, arithmetic and copies ran while one was open for 20% -> 20% of each run, Pallas kernels for 0% -> 0%
where the time goes in v1:
time: 1240 us; the launch traced here: 1220 us
  waiting for transfers between devices  531 us (43%)
  matrix products  192 us (15%)
  blocking collectives  159 us (13%)
  other arithmetic  154 us (12%)
  local copies, waits for them, and re-layouts  138 us (11%)
  loops' own time  21.5 us (2%)
  between operations  18 us (1%)
    select_n x64, other arithmetic, lap(): return jax.tree.map(lambda a, b: jnp.where(reached, a, b), new, before)  103 us
    dynamic_slice x96, local copies, waits for them, and re-layouts, lap(): new = combine(before, jax.tree.map(lambda part: part[at], everything))  100 us
    psum x1, waiting for transfers between devices, body(): lax.psum((grad_ln1_gain, grad_ln1_shift, grad_qkv_bias, grad_feat_query,...  95.3 us
    reduce_scatter x1, waiting for transfers between devices, body(): lax.psum_scatter(grad_down_full, ('fsdp', 'context'), scatter_dimension=1...  79.3 us
    reduce_scatter x1, waiting for transfers between devices, body(): lax.psum_scatter(grad_qkv_full, ('fsdp', 'context'), scatter_dimension=0,...  71.5 us
    all_gather x2, blocking collectives, entering(): everything = jax.tree.map(lambda part: lax.all_gather(part, axis), x)  67.4 us
    psum x1, blocking collectives, body(): lax.psum((grad_ln1_gain, grad_ln1_shift, grad_qkv_bias, grad_feat_query,...  59.3 us
    all_gather x1, waiting for transfers between devices, body(): lax.all_gather(up_weight, ('fsdp', 'context'), axis=0, tiled=True)  47.2 us
  transfers between devices with their start and end apart: 17, of which 11 were waited for; matrix products, arithmetic and copies ran while one was open for 20% of the time, Pallas kernels for 0%

profile of v1, /device:TPU:0, one launch (start us, length us, event | category | flops | bytes accessed | tf_op | source)
XLA Modules:
  0.0 1222.8 jit_solution(16137818308040176953)
XLA Ops:
  13.3 47.0 %all-gather.15.cloned.1.call-done = f32[768,3,384]{2,0,1:T(8,128)} async-done(((f32[48,3,384]{2,0,1:T(8,128)}), f32[768,3,384]{2,0,1:T(8,128)}) %all-gather.15.cloned.1.call-update) | async-done | bytes 3538960 | tf_op jit(solution)/shard_map/all_gather | solution.py:154
  60.3 8.5 convolution_add_fusion.1
  82.3 32.8 %all-reduce = f32[16]{0:T(128)} all-reduce(f32[16]{0:T(128)S(1)} %dynamic-update-slice), channel_id=1, replica_groups=mesh['fsdp'=4,'context'=4,'tensor'=2] {'fsdp','context'}, use_global_device_ids=true, to_apply=%add | all-reduce | flops 16 | bytes 128
  119.9 32.1 %all-gather.5 = f32[16,6,128]{2,1,0:T(8,128)} all-gather(f32[1,6,128]{2,1,0:T(8,128)S(1)} %bitcast.198), channel_id=3, replica_groups=mesh['fsdp'=4,'context'=4,'tensor'=2] {'fsdp','context'}, dimensions={0}, use_global_device_ids=true | all-gather | bytes 52224 | tf_op jit(solution)/shard_map/all_gather | solution.py:13
  155.7 8.0 multiply_reduce_fusion
  163.7 112.8 %while.22 = (s32[]{:T(128)}, f32[6,128,64]{2,1,0:T(8,128)}, f32[6,128]{1,0:T(8,128)}, s32[]{:T(128)}, f32[16,6,128,64]{2,3,1,0:T(8,128)}, /*index=5*/f32[16]{0:T...) while((s32[]{:T(128)}, f32[6,128,64]{2,1,0:T(8,128)}, f32[6,128]{1,0:T(8,128)}, ...), condition=%wide.region_15.16_spmd.clone, body=%wide.region_14.15_spmd.clone.sunk | while | flops 199685 | bytes 1385643 | solution.py:24
  281.7 6.3 fusion.59
  288.1 6.6 fusion.167
  300.9 33.7 %all-to-all-done.1 = f32[8,64,768]{2,1,0:T(8,128)S(1)} async-done(((f32[8,64,768]{2,1,0:T(8,128)}), f32[8,64,768]{2,1,0:T(8,128)S(1)}, u32[]{:S(2)}, u32[]{:S(2)}) %all-to-all-start.1) | async-done | bytes 1572896 | tf_op jit(solution)/shard_map/all_to_all | solution.py:203
  340.1 11.4 fusion.168
  353.6 47.2 %all-gather.19.cloned.1.call-done = f32[768,1536]{1,0:T(8,128)} async-done(((f32[48,1536]{1,0:T(8,128)}), f32[768,1536]{1,0:T(8,128)}) %all-gather.19.cloned.1.call-update) | async-done | bytes 4718608 | tf_op jit(solution)/shard_map/all_gather | solution.py:156
  400.8 14.7 %fusion.155 = (f32[1536]{0:T(1024)}, f32[512,1536]{1,0:T(8,128)S(1)}, f32[512,1536]{1,0:T(8,128)}) fusion(f32[512,1536]{1,0:T(8,128)} %fusion.168, f32[1536]{0:T(1024)S(1)} %copy-done.113, f32[768,1536]{1,0:T(8,128)} %all-gather.19.cloned.1.call-done, f32[512,768]{1,0:T(8,128)S(1)} %get-tuple-element.629, f32[768]{0:T(1024)S(1)} %copy-done.81, ...), kind=kOutput, calls=%fused_computation.257 | convolution fusion | flops 7265843712 | bytes 15751168 | tf_op jit(solution)/shard_map/dot_general | solution.py:52
  417.1 9.0 fusion.169
  426.2 12.4 %fusion.38 = f32[512,768]{1,0:T(8,128)} fusion(f32[1536,768]{0,1:T(8,128)} %all-gather.21.cloned.1.call-done, f32[512,1536]{1,0:T(8,128)} %get-tuple-element.657), kind=kOutput, calls=%fused_computation.80 | convolution fusion | flops 7254048768 | bytes 9437184 | tf_op jit(solution)/shard_map/dot_general | solution.py:53
  438.6 37.8 %all-reduce.10.cloned.1.call-done = f32[512,768]{1,0:T(8,128)} async-done(((f32[512,768]{1,0:T(8,128)}), f32[512,768]{1,0:T(8,128)}) %all-reduce.10.cloned.1.call-update) | async-done | bytes 1572880 | tf_op jit(solution)/shard_map/psum | solution.py:214
  479.0 43.9 %all-gather.25.cloned.1.call-done = f32[1024,768]{1,0:T(8,128)} async-done(((f32[512,768]{1,0:T(8,128)}), f32[1024,768]{1,0:T(8,128)}) %all-gather.25.cloned.1.call-update) | async-done | bytes 3145744 | tf_op jit(solution)/shard_map/all_gather | solution.py:195
  546.0 35.2 %all-gather.6 = f32[16,6,128]{2,1,0:T(8,128)} all-gather(f32[1,6,128]{2,1,0:T(8,128)S(1)} %fusion.126), channel_id=6, replica_groups=mesh['fsdp'=4,'context'=4,'tensor'=2] {'fsdp','context'}, dimensions={0}, use_global_device_ids=true | all-gather | bytes 52224 | tf_op jit(solution)/shard_map/all_gather | solution.py:13
  584.5 112.2 %while.23 = (s32[]{:T(128)}, f32[6,128,64]{2,1,0:T(8,128)}, f32[6,128]{1,0:T(8,128)}, s32[]{:T(128)}, f32[16,6,128,64]{2,3,1,0:T(8,128)}, /*index=5*/f32[16]{0:T...) while((s32[]{:T(128)}, f32[6,128,64]{2,1,0:T(8,128)}, ...), condition=%wide.region_31.33_spmd.clone, body=%wide.region_30.32_spmd.clone.sunk | while | flops 199689 | bytes 1385705 | solution.py:24
  702.7 7.3 fusion.171
  715.2 5.4 fusion.12
  720.6 8.8 fusion.13
  759.6 10.4 convolution_bitcast_fusion
  770.1 5.4 fusion.172
  775.6 11.9 fusion.62
  788.9 11.5 fusion.37
  807.0 9.5 fusion.30
  830.3 39.9 %all-to-all-done = f32[8,64,768]{2,1,0:T(8,128)} async-done(((f32[8,64,768]{2,1,0:T(8,128)}), f32[8,64,768]{2,1,0:T(8,128)}, u32[]{:S(2)}, u32[]{:S(2)}) %all-to-all-start) | async-done | bytes 1572896 | tf_op jit(solution)/shard_map/all_to_all | solution.py:198
  874.8 59.3 %all-reduce.1 = (f32[3]{0:T(128)S(1)}, f32[768]{0:T(1024)}, f32[768]{0:T(1024)}, f32[3,384]{1,0:T(4,128)}, f32[768]{0:T(1024)}, /*index=5*/f32[768]{0:T(1024)}, f32[768]{0:T(1024)}, f32[1536]{0:T(1024)}, f32[768]{0:T(1024)}) all-reduce(f32[3]{0:T(128)S(1)} %pad_maximum_fusion.5, ...), channel_id=1, replica_groups=mesh['fsdp'=4,'context'=4,'tensor'=2] {'fsdp','context'}, use_global_device_ids=true, to_apply=%region_25.27 | all-reduce | flops 7299 | bytes 58392 | tf_op jit(solution)/shard_map/psum | solution.py:258
  937.5 29.1 %reduce-scatter.9.cloned.1.call-done = f32[48,1536]{1,0:T(8,128)} async-done(((f32[768,1536]{1,0:T(8,128)}), f32[48,1536]{1,0:T(8,128)}) %reduce-scatter.9.cloned.1.call-update) | async-done | bytes 294928 | tf_op jit(solution)/shard_map/reduce_scatter | solution.py:255
  966.6 79.3 %reduce-scatter.11.cloned.1.call-done = f32[1536,48]{0,1:T(8,128)} async-done(((f32[1536,768]{0,1:T(8,128)}), f32[1536,48]{0,1:T(8,128)}) %reduce-scatter.11.cloned.1.call-update) | async-done | bytes 294928 | tf_op jit(solution)/shard_map/reduce_scatter | solution.py:256
  1045.9 95.3 %all-reduce.14.cloned.1.call-done = (f32[6,64,64]{2,1,0:T(8,128)}, f32[6,64,64]{2,1,0:T(8,128)}) async-done(((f32[6,64,64]{2,1,0:T(8,128)}, f32[6,64,64]{2,1,0:T(8,128)}), (f32[6,64,64]{2,1,0:T(8,128)}, f32[6,64,64]{2,1,0:T(8,128)})) %all-reduce.14.cloned.1.call-update) | async-done | bytes 196624 | tf_op jit(solution)/shard_map/psum | solution.py:258
  1141.1 71.5 %reduce-scatter.5.cloned.1.call-done = f32[48,3,384]{2,0,1:T(8,128)} async-done(((f32[768,3,384]{2,0,1:T(8,128)}), f32[48,3,384]{2,0,1:T(8,128)}) %reduce-scatter.5.cloned.1.call-update) | async-done | bytes 221200 | tf_op jit(solution)/shard_map/reduce_scatter | solution.py:253
  (551 shorter events, 352.2 us)
Async XLA Ops:
  7.2 62.7 %copy-start = (f32[6,64,64]{2,1,0:T(8,128)S(1)}, f32[6,64,64]{2,1,0:T(8,128)}, u32[]{:S(2)}) copy-start(f32[6,64,64]{2,1,0:T(8,128)} %param.31) | copy-start | bytes 294916
  7.2 53.1 %all-gather.15.cloned.1.call-start = ((), (), s32[]{:S(2)}) async-start(), calls=%async_computation.6 | async-start | bytes 3760128 | tf_op jit(solution)/shard_map/all_gather | solution.py:154
  8.0 155.7 %all-gather.23.cloned.1.call-start = ((), (), s32[]{:S(2)}) async-start(), calls=%async_computation.17 | async-start | bytes 3342336 | tf_op jit(solution)/shard_map/all_gather | solution.py:13
  8.8 70.6 %copy-start.109 = (s32[4,1]{0,1:T(1,128)}, s32[4,1]{0,1:T(1,128)S(1)}, u32[]{:S(2)}) copy-start(s32[4,1]{0,1:T(1,128)S(1)} %reduce-window.4) | copy-start | bytes 52
  8.8 51.4 %copy-start.107 = (f32[768]{0:T(1024)S(1)}, f32[768]{0:T(1024)}, u32[]{:S(2)}) copy-start(f32[768]{0:T(1024)} %param.27) | copy-start | bytes 9220
  8.8 51.4 %copy-start.114 = (f32[3,384]{1,0:T(4,128)S(1)}, f32[3,384]{1,0:T(4,128)}, u32[]{:S(2)}) copy-start(f32[3,384]{1,0:T(4,128)} %param.29) | copy-start | bytes 13828
  10.5 67.7 %copy-start.77 = (s32[512]{0:T(512)}, s32[512]{0:T(512)S(1)}, u32[]{:S(2)}) copy-start(s32[512]{0:T(512)S(1)} %select_select_fusion) | copy-start | bytes 6148
  11.1 57.6 %copy-start.88 = (f32[512]{0:T(512)}, f32[512]{0:T(512)S(1)}, u32[]{:S(2)}) copy-start(f32[512]{0:T(512)S(1)} %broadcast_multiply_fusion.2) | copy-start | bytes 6148
  11.5 57.3 %copy-start.95 = (f32[512]{0:T(512)}, f32[512]{0:T(512)S(1)}, u32[]{:S(2)}) copy-start(f32[512]{0:T(512)S(1)} %fusion.133) | copy-start | bytes 6148
  13.3 140.5 %copy-start.73 = (f32[512]{0:T(512)}, f32[512]{0:T(512)S(1)}, u32[]{:S(2)}) copy-start(f32[512]{0:T(512)S(1)} %get-tuple-element.644) | copy-start | bytes 6148
  72.0 470.6 %copy-start.56 = (f32[512,6]{0,1:T(8,128)}, f32[512,6]{0,1:T(8,128)S(1)}, u32[]{:S(2)}) copy-start(f32[512,6]{0,1:T(8,128)S(1)} %get-tuple-element.647) | copy-start | bytes 36868
  76.8 211.2 %all-gather.17.cloned.1.call-start = ((), (), s32[]{:S(2)}) async-start(), calls=%async_computation.7 | async-start | bytes 1253376 | tf_op jit(solution)/shard_map/all_gather | solution.py:155
  77.6 262.5 %all-gather.21.cloned.1.call-start = ((), (), s32[]{:S(2)}) async-start(), calls=%async_computation.10 | async-start | bytes 5013504 | tf_op jit(solution)/shard_map/all_gather | solution.py:157
  78.1 273.4 %all-reduce.8.cloned.1.call-start = ((), (), s32[]{:S(2)}) async-start(), calls=%async_computation.8 | async-start | bytes 3145728 | tf_op jit(solution)/shard_map/psum | solution.py:181
  152.3 127.8 %copy-start.2 = (f32[512,6,64]{0,2,1:T(8,128)}, f32[512,6,64]{0,2,1:T(8,128)S(1)}, u32[]{:S(2)}) copy-start(f32[512,6,64]{0,2,1:T(8,128)S(1)} %get-tuple-element.660) | copy-start | bytes 2359300
  152.3 127.8 %copy-start.5 = (f32[512,6,64]{0,2,1:T(8,128)}, f32[512,6,64]{0,2,1:T(8,128)S(1)}, u32[]{:S(2)}) copy-start(f32[512,6,64]{0,2,1:T(8,128)S(1)} %get-tuple-element.661) | copy-start | bytes 2359300
  294.7 106.1 %all-gather.19.cloned.1.call-start = ((), (), s32[]{:S(2)}) async-start(), calls=%async_computation.9 | async-start | bytes 5013504 | tf_op jit(solution)/shard_map/all_gather | solution.py:156
  295.3 39.3 %all-to-all-start.1 = ((f32[8,64,768]{2,1,0:T(8,128)}), f32[8,64,768]{2,1,0:T(8,128)S(1)}, u32[]{:S(2)}, u32[]{:S(2)}) async-start(f32[8,64,768]{2,1,0:T(8,128)} %bitcast.192), calls=%async_computation.1 | async-start | bytes 3145728 | tf_op jit(solution)/shard_map/all_to_all | solution.py:203
  298.9 177.5 %all-reduce.10.cloned.1.call-start = ((), (), s32[]{:S(2)}) async-start(), calls=%async_computation.11 | async-start | bytes 3145728 | tf_op jit(solution)/shard_map/psum | solution.py:214
  353.3 173.0 %copy-start.79 = (f32[512]{0:T(512)}, f32[512]{0:T(512)S(1)}, u32[]{:S(2)}) copy-start(f32[512]{0:T(512)S(1)} %broadcast_multiply_fusion.1) | copy-start | bytes 6148
  353.6 172.7 %copy-start.90 = (f32[512]{0:T(512)}, f32[512]{0:T(512)S(1)}, u32[]{:S(2)}) copy-start(f32[512]{0:T(512)S(1)} %fusion.134) | copy-start | bytes 6148
  426.1 96.7 %all-gather.25.cloned.1.call-start = ((), (), s32[]{:S(2)}) async-start(), calls=%async_computation.18 | async-start | bytes 4718592 | tf_op jit(solution)/shard_map/all_gather | solution.py:195
  438.6 145.9 %all-gather.27.cloned.1.call-start = ((), (), s32[]{:S(2)}) async-start(), calls=%async_computation.19 | async-start | bytes 3342336 | tf_op jit(solution)/shard_map/all_gather | solution.py:13
  538.8 333.8 %all-reduce.12.cloned.1.call-start = ((), (), s32[]{:S(2)}) async-start(), calls=%async_computation.12 | async-start | bytes 3145728 | tf_op jit(solution)/shard_map/psum | solution.py:248
  770.1 167.4 %reduce-scatter.7.cloned.1.call-start = ((), (), s32[]{:S(2)}) async-start(), calls=%async_computation.14 | async-start | bytes 1253376 | tf_op jit(solution)/shard_map/reduce_scatter | solution.py:254
  775.5 191.1 %reduce-scatter.9.cloned.1.call-start = ((), (), s32[]{:S(2)}) async-start(), calls=%async_computation.15 | async-start | bytes 5013504 | tf_op jit(solution)/shard_map/reduce_scatter | solution.py:255
  787.5 258.4 %reduce-scatter.11.cloned.1.call-start = ((), (), s32[]{:S(2)}) async-start(), calls=%async_computation.16 | async-start | bytes 5013504 | tf_op jit(solution)/shard_map/reduce_scatter | solution.py:256
  800.5 340.6 %all-reduce.14.cloned.1.call-start = ((), (), s32[]{:S(2)}) async-start(), calls=%async_computation.20 | async-start | bytes 786432 | tf_op jit(solution)/shard_map/psum | solution.py:258
  806.6 406.0 %reduce-scatter.5.cloned.1.call-start = ((), (), s32[]{:S(2)}) async-start(), calls=%async_computation.13 | async-start | bytes 3760128 | tf_op jit(solution)/shard_map/reduce_scatter | solution.py:253
  823.3 46.9 %all-to-all-start = ((f32[8,64,768]{2,1,0:T(8,128)}), f32[8,64,768]{2,1,0:T(8,128)}, u32[]{:S(2)}, u32[]{:S(2)}) async-start(f32[8,64,768]{2,1,0:T(8,128)} %broadcast_select_fusion.1), calls=%async_computation | async-start | bytes 3145728 | tf_op jit(solution)/shard_map/all_to_all | solution.py:198
  872.5 62.1 %copy-start.98 = (f32[512]{0:T(512)S(1)}, f32[512]{0:T(512)}, u32[]{:S(2)}) copy-start(f32[512]{0:T(512)} %copy-done.97) | copy-start | bytes 6148
  872.6 62.1 %copy-start.48 = (f32[512,768]{1,0:T(8,128)S(1)}, f32[512,768]{1,0:T(8,128)}, u32[]{:S(2)}) copy-start(f32[512,768]{1,0:T(8,128)} %all-reduce.12.cloned.1.call-done) | copy-start | bytes 4718596
  (104 other events, 760.4 us)
Sparse Core Ops, SparseCore 0:
  10.4 49.8 all-gather.14
  77.0 44.2 all-gather.22
  123.6 36.7 all-gather.16
  162.5 51.8 all-gather.20
  294.8 50.8 all-reduce.7
  347.8 52.9 all-gather.18
  426.3 50.0 all-reduce.9
  477.9 44.8 all-gather.24
  538.9 45.5 all-gather.26
  770.1 50.0 all-reduce.11
  824.4 63.1 reduce-scatter.6
  891.9 74.6 reduce-scatter.8
  971.0 74.7 reduce-scatter.10
  1050.3 90.7 all-reduce.13
  1145.4 67.1 reduce-scatter.4
